TPU v7x, 512 devices: a whole 4x8x8 slice. The times are simulated.
512 devices in a mesh: tm: 4 (over y_hi, core), pix: 128 (over x, z, y_lo).
Axes of the slice: x: 4, y: 8 (y_hi: 2, y_lo: 4; y = y_hi * 4 + y_lo), z: 8, core: 2. Of those that a mesh axis runs over, the one named last changes fastest.
Arguments:
- activations: bfloat16 [4, 327680, 256], P('tm', 'pix'), may hold values from -6 to 6
- down_weight: bfloat16 [1024, 256], replicated, may hold values from -0.1875 to 0.1875
- down_bias: float32 [256], replicated, may hold values from -3 to 3
- taps: float32 [9, 256], replicated, may hold values from -2 to 2
- point_weight: bfloat16 [256, 256], replicated, may hold values from -0.375 to 0.375
- time_mix: float32 [4, 4, 256], replicated, may hold values from -3 to 3
- edge_rows: int32 [128, 2, 20], P('pix'), may hold values from 0 to 19, as said below
- cotangent: bfloat16 [4, 81920, 256], P(None, ('pix', 'tm')), may hold values from -6 to 6
Outputs:
- grad_input: bfloat16 [4, 327680, 256], P('tm', 'pix')
- grad_down: float32 [1024, 256], replicated
- grad_bias: float32 [256], replicated
- grad_taps: float32 [9, 256], replicated
- grad_point: float32 [256, 256], replicated
- grad_mix: float32 [4, 4, 256], replicated
Inputs may be any that keep to these rules, and one draw needn't show every extreme that they name: Each edge_rows[t, e] is either 0, 1, .., 19 or its reversal; edge_rows[t, 1] equals edge_rows[(t + 1) mod 128, 0].
All inputs are finite; a program needn't handle non-finite values.
Results may differ from a plain program's by a relative error of at most 0.014.
Values may be sent and summed in bfloat16 or wider, within the bound.
No kernel may reach another device: no remote copies, remote signals or barrier semaphores. Data moves between devices by JAX's collectives and lax.ppermute only.
A program may use at most 64 MiB of HBM per device.

v0:
```python
import math
import jax
import jax.numpy as jnp
from jax import lax
from jax.sharding import Mesh, PartitionSpec as P

C = 256
TR = 20
TC = 32
TM = ("yh", "core")
PIX = ("x", "z", "yl")
RING = ("yh", "yl")
SUM_ROWS = 1306
PAD_ROWS = 1536


def padded_2(cells, sides, width):
    for axis, dim in sides:
        count = lax.axis_size(axis)
        head = lax.slice_in_dim(cells, 0, width, axis=dim)
        tail = lax.slice_in_dim(cells, cells.shape[dim] - width, cells.shape[dim], axis=dim)
        cells = jnp.concatenate(
            [
                lax.ppermute(tail, axis, [(i, (i + 1) % count) for i in range(count)]),
                cells,
                lax.ppermute(head, axis, [((i + 1) % count, i) for i in range(count)]),
            ],
            axis=dim,
        )
    return cells


def scatter_sum(rows, axis):
    count = lax.axis_size(axis)
    low = rows.astype(jnp.bfloat16).reshape(count, rows.shape[0] // count, C)
    got = lax.all_to_all(low, axis, split_axis=0, concat_axis=0, tiled=True)
    return jnp.sum(got.astype(jnp.float32), axis=0)


def copies(rows, axis):
    count = lax.axis_size(axis)
    wide = jnp.broadcast_to(rows[None], (count,) + rows.shape)
    return lax.all_to_all(wide, axis, split_axis=0, concat_axis=0, tiled=True)


def sum_over_devices(parts):
    half = PAD_ROWS // 2
    core = lax.axis_index("core")
    keep = lax.dynamic_slice_in_dim(parts, core * half, half, axis=0)
    send = lax.dynamic_slice_in_dim(parts, (1 - core) * half, half, axis=0)
    got = lax.ppermute(send.astype(jnp.bfloat16), "core", [(0, 1), (1, 0)])
    rows = keep + got.astype(jnp.float32)
    rows = scatter_sum(rows, "x")
    rows = scatter_sum(rows, "z")
    rows = jnp.sum(copies(rows.astype(jnp.bfloat16), RING).astype(jnp.float32), axis=0)
    rows = rows.astype(jnp.bfloat16)
    rows = copies(rows, "z").reshape(-1, C)
    rows = copies(rows, "x").reshape(-1, C)
    rows = lax.all_gather(rows, "core", axis=0, tiled=True)
    return rows.astype(jnp.float32)


def on_device(
    activations, down_weight, down_bias, taps, point_weight, time_mix, edge_rows, cotangent
):
    frames = lax.axis_size(TM)
    tiles = lax.axis_size(PIX)
    pixels = TR * TC
    scale = 1.0 / math.sqrt(frames * tiles * pixels)
    rows_in = activations.reshape(pixels, 4 * C)
    preact = jnp.dot(rows_in, down_weight, preferred_element_type=jnp.float32) + down_bias
    pooled = jax.nn.silu(preact).astype(jnp.bfloat16)
    tile_grid = pooled.reshape(1, TR, TC, C)
    padded = padded_2(tile_grid, ((PIX, 2),), 1)
    west_map = edge_rows[0, 0]
    east_map = edge_rows[0, 1]
    west_col = jnp.take(padded[0, :, 0, :], west_map, axis=0)
    east_col = jnp.take(padded[0, :, TC + 1, :], east_map, axis=0)
    widened = jnp.concatenate([west_col[:, None, :], tile_grid[0], east_col[:, None, :]], axis=1)
    widened = jnp.pad(widened, ((1, 1), (0, 0), (0, 0)))
    spread = jnp.zeros((TR, TC, C), jnp.float32)
    for row_off in range(3):
        for col_off in range(3):
            spread = (
                spread
                + taps[row_off * 3 + col_off]
                * widened[row_off : row_off + TR, col_off : col_off + TC, :]
            )
    spread_low = spread.astype(jnp.bfloat16).reshape(pixels, C)
    mixed_in = (
        pooled.astype(jnp.float32)
        + jnp.dot(spread_low, point_weight, preferred_element_type=jnp.float32)
    ).astype(jnp.bfloat16)
    by_pixel = lax.all_to_all(
        mixed_in.reshape(1, pixels, C), TM, split_axis=1, concat_axis=0, tiled=True
    )
    mix_part = jnp.einsum("gpc,fpc->fgc", by_pixel, cotangent, preferred_element_type=jnp.float32)
    cot_f = cotangent.astype(jnp.float32)
    mixed_acc = jnp.zeros((frames, cotangent.shape[1], C), jnp.float32)
    for source in range(frames):
        mixed_acc = mixed_acc + time_mix[source][:, None, :] * cot_f[source][None, :, :]
    mixed_grad = mixed_acc.astype(jnp.bfloat16)
    back_grad = lax.all_to_all(mixed_grad, TM, split_axis=0, concat_axis=1, tiled=True)
    mixed_rows = back_grad.reshape(pixels, C)
    point_part = jnp.dot(spread_low.T, mixed_rows, preferred_element_type=jnp.float32)
    spread_grad = jnp.dot(mixed_rows, point_weight.T, preferred_element_type=jnp.float32).astype(
        jnp.bfloat16
    )
    grad_float = spread_grad.reshape(TR, TC, C).astype(jnp.float32)
    taps_rows = []
    for row_off in range(3):
        for col_off in range(3):
            taps_rows.append(
                jnp.sum(
                    grad_float * widened[row_off : row_off + TR, col_off : col_off + TC, :],
                    axis=(0, 1),
                )
            )
    taps_part = jnp.stack(taps_rows, axis=0)
    grad_padded = jnp.pad(grad_float, ((2, 2), (2, 2), (0, 0)))
    wide_grad = jnp.zeros((TR + 2, TC + 2, C), jnp.float32)
    for row_off in range(3):
        for col_off in range(3):
            wide_grad = (
                wide_grad
                + taps[row_off * 3 + col_off]
                * grad_padded[2 - row_off : 4 - row_off + TR, 2 - col_off : 4 - col_off + TC, :]
            )
    west_back = jnp.take(wide_grad[1 : TR + 1, 0, :], west_map, axis=0)
    east_back = jnp.take(wide_grad[1 : TR + 1, TC + 1, :], east_map, axis=0)
    outgoing = jnp.stack([west_back, east_back], axis=1)
    incoming = padded_2(outgoing.astype(jnp.bfloat16), ((PIX, 1),), 1).astype(outgoing.dtype)
    inner_grad = wide_grad[1 : TR + 1, 1 : TC + 1, :]
    inner_grad = inner_grad.at[:, 0, :].add(incoming[:, 0, :])
    inner_grad = inner_grad.at[:, TC - 1, :].add(incoming[:, 3, :])
    pooled_grad = mixed_rows.astype(jnp.float32) + inner_grad.reshape(pixels, C)
    sigma = jax.nn.sigmoid(preact)
    pre_grad = (pooled_grad * (sigma * (1.0 + preact * (1.0 - sigma)))).astype(jnp.bfloat16)
    bias_part = jnp.sum(pre_grad.astype(jnp.float32), axis=0)
    down_part = jnp.dot(rows_in.T, pre_grad, preferred_element_type=jnp.float32)
    grad_input = jnp.dot(pre_grad, down_weight.T, preferred_element_type=jnp.float32).astype(
        jnp.bfloat16
    )
    parts = jnp.concatenate(
        [
            down_part,
            point_part,
            mix_part.reshape(frames * frames, C),
            taps_part,
            bias_part.reshape(1, C),
            jnp.zeros((PAD_ROWS - SUM_ROWS, C), jnp.float32),
        ],
        axis=0,
    )
    total = sum_over_devices(parts) * scale
    grad_down = total[:1024]
    grad_point = total[1024:1280]
    grad_mix = total[1280:1296].reshape(frames, frames, C)
    grad_taps = total[1296:1305]
    grad_bias = total[1305]
    return (
        grad_input.reshape(1, 4 * pixels, C),
        grad_down,
        grad_bias,
        grad_taps,
        grad_point,
        grad_mix,
    )


def solution(mesh):
    chips = Mesh(mesh.devices.reshape(2, 2, 4, 8, 4), ("yh", "core", "x", "z", "yl"))
    in_specs = (
        P(TM, PIX, None),
        P(),
        P(),
        P(),
        P(),
        P(),
        P(PIX, None, None),
        P(None, PIX + TM, None),
    )
    out_specs = (P(TM, PIX, None), P(), P(), P(), P(), P())
    return jax.shard_map(
        on_device, mesh=chips, in_specs=in_specs, out_specs=out_specs, check_vma=False
    )
```

profile of v0, /device:TPU:1, one launch (start us, length us, event | category | flops | bytes accessed | tf_op | source)
XLA Modules:
  0.0 167.9 jit_solution(9329589787763400051)
XLA Ops:
  0.6 0.8 slice_bitcast_fusion.9
  1.4 1.0 convert_element_type.105
  2.6 0.9 add_convert_fusion.1
  3.5 10.3 %all-to-all-start = ((bf16[4,160,256]{2,1,0:T(8,128)(2,1)}), bf16[4,160,256]{2,1,0:T(8,128)(2,1)S(1)}, u32[]{:S(2)}, u32[]{:S(2)}) async-start(bf16[4,160,256]{2,1,0:T(8,128)(2,1)} %add_convert_fusion.1), calls=%async_computation | async-start | bytes 655360 | tf_op jit(solution)/shard_map/all_to_all | solution.py:103
  13.8 9.8 %all-to-all-done = bf16[4,160,256]{2,1,0:T(8,128)(2,1)S(1)} async-done(((bf16[4,160,256]{2,1,0:T(8,128)(2,1)}), bf16[4,160,256]{2,1,0:T(8,128)(2,1)S(1)}, u32[]{:S(2)}, u32[]{:S(2)}) %all-to-all-start) | async-done | bytes 327712 | tf_op jit(solution)/shard_map/all_to_all | solution.py:103
  24.4 0.6 fusion.12
  24.9 0.9 copy-done.2
  25.8 0.6 gather_fusion.1
  26.5 11.3 %collective-permute-start.1 = (bf16[20,1,256]{2,0,1:T(8,128)(2,1)S(1)}, bf16[20,1,256]{2,0,1:T(8,128)(2,1)S(1)}, u32[]{:S(2)}, u32[]{:S(2)}) collective-permute-start(bf16[20,1,256]{2,0,1:T(8,128)(2,1)S(1)} %fusion.49), channel_id=1, source_target_pairs={{1,0},{2,1},{3,2},{4,3},{5,4},{6,5},{7,6},{8,7},{9,8},{10,9},{11,1... | collective-permute-start | bytes 30728 | tf_op jit(solution)/shard_map/ppermute | solution.py:26
  37.9 0.6 gather_fusion
  38.5 1.9 %collective-permute-start = (bf16[20,1,256]{2,0,1:T(8,128)(2,1)S(1)}, bf16[20,1,256]{2,0,1:T(8,128)(2,1)S(1)}, u32[]{:S(2)}, u32[]{:S(2)}) collective-permute-start(bf16[20,1,256]{2,0,1:T(8,128)(2,1)S(1)} %fusion.48), channel_id=1, source_target_pairs={{0,1},{1,2},{2,3},{3,4},{4,5},{5,6},{6,7},{7,8},{8,9},{9,10},{10,1... | collective-permute-start | bytes 30728 | tf_op jit(solution)/shard_map/ppermute | solution.py:24
  40.5 1.0 copy.110
  41.5 2.5 %reshape.148 = bf16[640,1024]{1,0:T(8,128)(2,1)S(1)} reshape(bf16[1,2560,256]{2,1,0:T(8,128)(2,1)} %param.16) | data formatting | bytes 2621440 | tf_op jit(solution)/shard_map/reshape | solution.py:70
  44.0 1.2 slice.277
  45.3 3.7 %collective-permute-done = bf16[20,1,256]{2,0,1:T(8,128)(2,1)S(1)} collective-permute-done((bf16[20,1,256]{2,0,1:T(8,128)(2,1)S(1)}, bf16[20,1,256]{2,0,1:T(8,128)(2,1)S(1)}, u32[]{:S(2)}, u32[]{:S(2)}) %collective-permute-start) | collective-permute-done | bytes 10272 | tf_op jit(solution)/shard_map/ppermute | solution.py:24
  49.0 0.7 fusion.47
  50.0 0.8 fusion.38
  50.8 5.7 %collective-permute-start.3 = (bf16[1,20,1,256]{3,1,2,0:T(8,128)(2,1)S(1)}, bf16[1,20,1,256]{3,1,2,0:T(8,128)(2,1)S(1)}, u32[]{:S(2)}, u32[]{:S(2)}) collective-permute-start(bf16[1,20,1,256]{3,1,2,0:T(8,128)(2,1)S(1)} %copy.128), channel_id=1, source_target_pairs={{1,0},{2,1},{3,2},{4,3},{5,4},{6,5},{7,6},{8,7},{9,8},{10,9},{11,1... | collective-permute-start | bytes 30728 | tf_op jit(solution)/shard_map/ppermute | solution.py:26
  56.5 1.9 %collective-permute-start.2 = (bf16[1,20,1,256]{3,1,2,0:T(8,128)(2,1)S(1)}, bf16[1,20,1,256]{3,1,2,0:T(8,128)(2,1)S(1)}, u32[]{:S(2)}, u32[]{:S(2)}) collective-permute-start(bf16[1,20,1,256]{3,1,2,0:T(8,128)(2,1)S(1)} %copy.127), channel_id=1, source_target_pairs={{0,1},{1,2},{2,3},{3,4},{4,5},{5,6},{6,7},{7,8},{8,9},{9,10},{10,1... | collective-permute-start | bytes 30728 | tf_op jit(solution)/shard_map/ppermute | solution.py:24
  58.4 1.6 convolution_bitcast_fusion
  60.0 0.8 copy.123
  60.8 0.8 copy.118
  61.6 0.6 gather_fusion.3
  62.2 4.8 %collective-permute-done.2 = bf16[1,20,1,256]{3,1,2,0:T(8,128)(2,1)S(1)} collective-permute-done((bf16[1,20,1,256]{3,1,2,0:T(8,128)(2,1)S(1)}, bf16[1,20,1,256]{3,1,2,0:T(8,128)(2,1)S(1)}, u32[]{:S(2)}, u32[]{:S(2)}) %collective-permute-start.2) | collective-permute-done | bytes 10272 | tf_op jit(solution)/shard_map/ppermute | solution.py:24
  67.0 0.6 gather_fusion.2
  67.9 0.8 fusion.29
  68.9 0.5 copy.130
  69.4 0.5 broadcast.133
  70.0 3.4 %reduce.8 = bf16[640,256]{1,0:T(8,128)(2,1)} reduce(bf16[640,1,256]{2,1,0:T(2,128)(2,1)S(1)} %bitcast.109, bf16[]{:T(256)} %broadcast.133), dimensions={1}, to_apply=%bitcast.98.reduce_sub_computation | reduce | bytes 655362
  73.4 1.8 %reshape.204 = bf16[4,2,20480]{2,1,0:T(2,128)(2,1)} reshape(bf16[640,256]{1,0:T(8,128)(2,1)} %reduce.8) | data formatting | bytes 655360
  75.1 6.4 %all-to-all-start.1 = ((bf16[4,2,20480]{2,1,0:T(2,128)(2,1)}), bf16[4,2,20480]{2,1,0:T(2,128)(2,1)S(1)}, u32[]{:S(2)}, u32[]{:S(2)}) async-start(bf16[4,2,20480]{2,1,0:T(2,128)(2,1)} %reshape.204), calls=%async_computation.1 | async-start | bytes 655360 | tf_op jit(solution)/shard_map/all_to_all | solution.py:94
  81.5 0.7 fusion.37
  82.2 0.8 copy.121
  83.0 0.8 copy.122
  83.8 0.8 copy.120
  84.6 0.8 copy.116
  85.4 0.8 copy.115
  86.2 0.8 copy.114
  87.0 0.8 copy.117
  87.8 0.8 copy.119
  88.6 1.0 fusion.53
  89.6 1.7 %all-to-all-done.1 = bf16[4,2,20480]{2,1,0:T(2,128)(2,1)S(1)} async-done(((bf16[4,2,20480]{2,1,0:T(2,128)(2,1)}), bf16[4,2,20480]{2,1,0:T(2,128)(2,1)S(1)}, u32[]{:S(2)}, u32[]{:S(2)}) %all-to-all-start.1) | async-done | bytes 327712 | tf_op jit(solution)/shard_map/all_to_all | solution.py:94
  91.7 1.1 copy.109
  92.8 1.5 convolution_bitcast_fusion.1
  94.5 0.8 copy.113
  95.3 0.7 broadcast_in_dim.49
  96.0 3.0 %concatenate.24 = f32[1536,256]{0,1:T(8,128)S(1)} concatenate(f32[1024,256]{0,1:T(8,128)S(1)} %copy-done.1, f32[256,256]{0,1:T(8,128)S(1)} %copy-done.6, f32[16,256]{0,1:T(8,128)} %copy.113, f32[1,256]{0,1:T(8,128)} %copy.114, f32[1,256]{0,1:T(8,128)} %copy.115, f32[1,256]{0,1:T(8,128)} %copy.116, f32[1,256]{0,1:T(8,128)} %copy.117, f32[1,256]{0,1:T(8,128)} %copy.118, ...), dimensions={0} | concatenate | bytes 3145728 | tf_op jit(solution)/shard_map/concatenate | solution.py:144
  99.1 2.8 %collective-permute-start.4 = (bf16[768,256]{0,1:T(8,128)(2,1)S(1)}, bf16[768,256]{0,1:T(8,128)(2,1)S(1)}, u32[]{:S(2)}, u32[]{:S(2)}) collective-permute-start(bf16[768,256]{0,1:T(8,128)(2,1)S(1)} %dynamic-slice_convert_fusion), channel_id=1, source_target_pairs={{0,128},{128,0},{1,129},{129,1},{2,130},{130,2},{3,131},{131,3},{4... | collective-permute-start | bytes 1179656 | tf_op jit(solution)/shard_map/ppermute | solution.py:51
  101.9 1.3 collective-permute-done.4
  103.5 10.2 %all_to_all.46 = bf16[4,192,256]{2,1,0:T(8,128)(2,1)S(1)} all-to-all(bf16[4,192,256]{2,1,0:T(8,128)(2,1)S(1)} %bitcast.111), channel_id=1, replica_groups=mesh['yh'=2,'core'=2,'x'=4,'z'=8,'yl'=4] {'x'}, dimensions={0} | all-to-all | bytes 786432 | tf_op jit(solution)/shard_map/all_to_all | solution.py:36
  113.8 10.2 %all_to_all.47 = bf16[8,24,256]{2,1,0:T(8,128)(2,1)S(1)} all-to-all(bf16[8,24,256]{2,1,0:T(8,128)(2,1)S(1)} %bitcast.116), channel_id=1, replica_groups=mesh['yh'=2,'core'=2,'x'=4,'z'=8,'yl'=4] {'z'}, dimensions={0} | all-to-all | bytes 196608 | tf_op jit(solution)/shard_map/all_to_all | solution.py:36
  124.0 11.8 %all_to_all.48 = bf16[8,24,256]{2,1,0:T(8,128)(2,1)S(1)} all-to-all(bf16[8,24,256]{2,1,0:T(8,128)(2,1)S(1)} %broadcast_in_dim.50), channel_id=1, replica_groups=mesh['yh'=2,'core'=2,'x'=4,'z'=8,'yl'=4] {'yh','yl'}, dimensions={0} | all-to-all | bytes 196608 | tf_op jit(solution)/shard_map/all_to_all | solution.py:43
  135.8 10.0 %all_to_all.49 = bf16[8,24,256]{2,1,0:T(8,128)(2,1)S(1)} all-to-all(bf16[8,24,256]{2,1,0:T(8,128)(2,1)S(1)} %broadcast_in_dim.51), channel_id=1, replica_groups=mesh['yh'=2,'core'=2,'x'=4,'z'=8,'yl'=4] {'z'}, dimensions={0} | all-to-all | bytes 196608 | tf_op jit(solution)/shard_map/all_to_all | solution.py:43
  145.8 0.8 broadcast_in_dim.53
  146.6 3.5 %all-to-all-start.6 = ((bf16[4,192,256]{2,1,0:T(8,128)(2,1)}), bf16[4,192,256]{2,1,0:T(8,128)(2,1)S(1)}, u32[]{:S(2)}, u32[]{:S(2)}) async-start(bf16[4,192,256]{2,1,0:T(8,128)(2,1)} %broadcast_in_dim.53), calls=%async_computation.6 | async-start | bytes 786432 | tf_op jit(solution)/shard_map/all_to_all | solution.py:43
  150.0 0.5 convolution_convert_fusion
  150.6 1.6 reshape.149
  152.2 4.0 %all-to-all-done.6 = bf16[4,192,256]{2,1,0:T(8,128)(2,1)S(1)} async-done(((bf16[4,192,256]{2,1,0:T(8,128)(2,1)}), bf16[4,192,256]{2,1,0:T(8,128)(2,1)S(1)}, u32[]{:S(2)}, u32[]{:S(2)}) %all-to-all-start.6) | async-done | bytes 393248 | tf_op jit(solution)/shard_map/all_to_all | solution.py:43
  156.2 8.0 %all_gather.3 = bf16[1536,256]{1,0:T(8,128)(2,1)S(1)} all-gather(bf16[768,256]{1,0:T(8,128)(2,1)S(1)} %bitcast.112), channel_id=1, replica_groups=mesh['yh'=2,'core'=2,'x'=4,'z'=8,'yl'=4] {'core'}, dimensions={0}, use_global_device_ids=true | all-gather | bytes 1179648 | tf_op jit(solution)/shard_map/all_gather | solution.py:59
  164.3 0.6 slice.291
  164.9 0.6 slice.292
  165.5 0.7 slice.293
  166.2 1.0 slice.290
  167.3 0.6 reshape.158
  (59 shorter events, 3.0 us)
Async XLA Ops:
  0.6 49.3 %copy-start = (bf16[1024,256]{1,0:T(8,128)(2,1)S(1)}, bf16[1024,256]{1,0:T(8,128)(2,1)}, u32[]{:S(2)}) copy-start(bf16[1024,256]{1,0:T(8,128)(2,1)} %param.17) | copy-start | bytes 1572868
  2.5 11.3 %copy-start.10 = (s32[1,2,20]{2,1,0:T(2,128)S(1)}, s32[1,2,20]{2,1,0:T(2,128)}, u32[]{:S(2)}) copy-start(s32[1,2,20]{2,1,0:T(2,128)} %param.22) | copy-start | bytes 484
  2.5 11.3 %copy-start.9 = (f32[9,256]{1,0:T(8,128)S(1)}, f32[9,256]{1,0:T(8,128)}, u32[]{:S(2)}) copy-start(f32[9,256]{1,0:T(8,128)} %param.19) | copy-start | bytes 27652
  2.5 21.2 %copy-start.7 = (bf16[256,256]{1,0:T(8,128)(2,1)S(1)}, bf16[256,256]{1,0:T(8,128)(2,1)}, u32[]{:S(2)}) copy-start(bf16[256,256]{1,0:T(8,128)(2,1)} %param.20) | copy-start | bytes 393220
  3.5 20.2 %all-to-all-start = ((bf16[4,160,256]{2,1,0:T(8,128)(2,1)}), bf16[4,160,256]{2,1,0:T(8,128)(2,1)S(1)}, u32[]{:S(2)}, u32[]{:S(2)}) async-start(bf16[4,160,256]{2,1,0:T(8,128)(2,1)} %add_convert_fusion.1), calls=%async_computation | async-start | bytes 655360 | tf_op jit(solution)/shard_map/all_to_all | solution.py:103
  24.3 16.1 %copy-start.3 = (bf16[4,160,256]{2,1,0:T(8,128)(2,1)S(1)}, bf16[4,160,256]{2,1,0:T(8,128)(2,1)}, u32[]{:S(2)}) copy-start(bf16[4,160,256]{2,1,0:T(8,128)(2,1)} %param.23) | copy-start | bytes 983044
  24.9 0.9 copy-start.2
  26.5 18.7 %collective-permute-start.1 = (bf16[20,1,256]{2,0,1:T(8,128)(2,1)S(1)}, bf16[20,1,256]{2,0,1:T(8,128)(2,1)S(1)}, u32[]{:S(2)}, u32[]{:S(2)}) collective-permute-start(bf16[20,1,256]{2,0,1:T(8,128)(2,1)S(1)} %fusion.49), channel_id=1, source_target_pairs={{1,0},{2,1},{3,2},{4,3},{5,4},{6,5},{7,6},{8,7},{9,8},{10,9},{11,1... | collective-permute-start | bytes 30728 | tf_op jit(solution)/shard_map/ppermute | solution.py:26
  38.5 10.4 %collective-permute-start = (bf16[20,1,256]{2,0,1:T(8,128)(2,1)S(1)}, bf16[20,1,256]{2,0,1:T(8,128)(2,1)S(1)}, u32[]{:S(2)}, u32[]{:S(2)}) collective-permute-start(bf16[20,1,256]{2,0,1:T(8,128)(2,1)S(1)} %fusion.48), channel_id=1, source_target_pairs={{0,1},{1,2},{2,3},{3,4},{4,5},{5,6},{6,7},{7,8},{8,9},{9,10},{10,1... | collective-permute-start | bytes 30728 | tf_op jit(solution)/shard_map/ppermute | solution.py:24
  44.0 5.9 %copy-start.11 = (f32[256]{0:T(256)S(1)}, f32[256]{0:T(256)}, u32[]{:S(2)}) copy-start(f32[256]{0:T(256)} %param.18) | copy-start | bytes 3076
  50.8 9.3 %copy-start.4 = (bf16[640,256]{1,0:T(8,128)(2,1)}, bf16[640,256]{1,0:T(8,128)(2,1)S(1)}, u32[]{:S(2)}) copy-start(bf16[640,256]{1,0:T(8,128)(2,1)S(1)} %get-tuple-element.53) | copy-start | bytes 983044
  50.8 10.8 %collective-permute-start.3 = (bf16[1,20,1,256]{3,1,2,0:T(8,128)(2,1)S(1)}, bf16[1,20,1,256]{3,1,2,0:T(8,128)(2,1)S(1)}, u32[]{:S(2)}, u32[]{:S(2)}) collective-permute-start(bf16[1,20,1,256]{3,1,2,0:T(8,128)(2,1)S(1)} %copy.128), channel_id=1, source_target_pairs={{1,0},{2,1},{3,2},{4,3},{5,4},{6,5},{7,6},{8,7},{9,8},{10,9},{11,1... | collective-permute-start | bytes 30728 | tf_op jit(solution)/shard_map/ppermute | solution.py:26
  56.5 10.5 %collective-permute-start.2 = (bf16[1,20,1,256]{3,1,2,0:T(8,128)(2,1)S(1)}, bf16[1,20,1,256]{3,1,2,0:T(8,128)(2,1)S(1)}, u32[]{:S(2)}, u32[]{:S(2)}) collective-permute-start(bf16[1,20,1,256]{3,1,2,0:T(8,128)(2,1)S(1)} %copy.127), channel_id=1, source_target_pairs={{0,1},{1,2},{2,3},{3,4},{4,5},{5,6},{6,7},{7,8},{8,9},{9,10},{10,1... | collective-permute-start | bytes 30728 | tf_op jit(solution)/shard_map/ppermute | solution.py:24
  75.1 16.2 %all-to-all-start.1 = ((bf16[4,2,20480]{2,1,0:T(2,128)(2,1)}), bf16[4,2,20480]{2,1,0:T(2,128)(2,1)S(1)}, u32[]{:S(2)}, u32[]{:S(2)}) async-start(bf16[4,2,20480]{2,1,0:T(2,128)(2,1)} %reshape.204), calls=%async_computation.1 | async-start | bytes 655360 | tf_op jit(solution)/shard_map/all_to_all | solution.py:94
  89.6 3.1 %copy-start.8 = (bf16[4,160,256]{1,0,2:T(4,128)(2,1)S(1)}, bf16[4,160,256]{1,0,2:T(4,128)(2,1)}, u32[]{:S(2)}) copy-start(bf16[4,160,256]{1,0,2:T(4,128)(2,1)} %copy.110) | copy-start | bytes 983044
  92.8 3.3 %copy-start.1 = (f32[1024,256]{0,1:T(8,128)S(1)}, f32[1024,256]{0,1:T(8,128)}, u32[]{:S(2)}) copy-start(f32[1024,256]{0,1:T(8,128)} %convolution_bitcast_fusion) | copy-start | bytes 3145732
  92.8 3.3 %copy-start.6 = (f32[256,256]{0,1:T(8,128)S(1)}, f32[256,256]{0,1:T(8,128)}, u32[]{:S(2)}) copy-start(f32[256,256]{0,1:T(8,128)} %fusion.53) | copy-start | bytes 786436
  99.1 4.1 %collective-permute-start.4 = (bf16[768,256]{0,1:T(8,128)(2,1)S(1)}, bf16[768,256]{0,1:T(8,128)(2,1)S(1)}, u32[]{:S(2)}, u32[]{:S(2)}) collective-permute-start(bf16[768,256]{0,1:T(8,128)(2,1)S(1)} %dynamic-slice_convert_fusion), channel_id=1, source_target_pairs={{0,128},{128,0},{1,129},{129,1},{2,130},{130,2},{3,131},{131,3},{4... | collective-permute-start | bytes 1179656 | tf_op jit(solution)/shard_map/ppermute | solution.py:51
  113.7 36.3 %copy-start.5 = (bf16[640,256]{1,0:T(8,128)(2,1)S(1)}, bf16[640,256]{1,0:T(8,128)(2,1)}, u32[]{:S(2)}) copy-start(bf16[640,256]{1,0:T(8,128)(2,1)} %copy-done.4) | copy-start | bytes 983044
  146.6 9.7 %all-to-all-start.6 = ((bf16[4,192,256]{2,1,0:T(8,128)(2,1)}), bf16[4,192,256]{2,1,0:T(8,128)(2,1)S(1)}, u32[]{:S(2)}, u32[]{:S(2)}) async-start(bf16[4,192,256]{2,1,0:T(8,128)(2,1)} %broadcast_in_dim.53), calls=%async_computation.6 | async-start | bytes 786432 | tf_op jit(solution)/shard_map/all_to_all | solution.py:43
where the time goes:
time: 169 us; the launch traced here: 168 us
  blocking collectives  50.1 us (30%)
  starting transfers between devices  43.8 us (26%)
  local copies, waits for them, and re-layouts  32.7 us (19%)
  waiting for transfers between devices  25.4 us (15%)
  other arithmetic  8.94 us (5%)
  matrix products  5.94 us (4%)
    all_to_all x2, blocking collectives, copies(): return lax.all_to_all(wide, axis, split_axis=0, concat_axis=0, tiled=True)  21.7 us
    all_to_all x2, blocking collectives, scatter_sum(): got = lax.all_to_all(low, axis, split_axis=0, concat_axis=0, tiled=True)  20.4 us
    ppermute x2, starting transfers between devices, padded_2(): lax.ppermute(head, axis, [((i + 1) % count, i) for i in range(count)])  17 us
    all_to_all x1, starting transfers between devices, on_device(): lax.all_to_all(mixed_grad, TM, split_axis=0, concat_axis=1, tiled=True)  10.3 us
    all_to_all x1, waiting for transfers between devices, on_device(): lax.all_to_all(mixed_grad, TM, split_axis=0, concat_axis=1, tiled=True)  9.85 us
    ppermute x2, waiting for transfers between devices, padded_2(): lax.ppermute(tail, axis, [(i, (i + 1) % count) for i in range(count)])  8.5 us
    all_gather x1, blocking collectives, sum_over_devices(): rows = lax.all_gather(rows, 'core', axis=0, tiled=True)  7.95 us
    another operation x9, local copies, waits for them, and re-layouts, on_device(): taps_part = jnp.stack(taps_rows, axis=0)  7.14 us
  transfers between devices with their start and end apart: 8, of which 6 were waited for; matrix products, arithmetic and copies ran while one was open for 12% of the time, Pallas kernels for 0%

commit v1 on v0

--- a/solution.py
+++ b/solution.py
@@ -100,7 +100,10 @@
     for source in range(frames):
         mixed_acc = mixed_acc + time_mix[source][:, None, :] * cot_f[source][None, :, :]
     mixed_grad = mixed_acc.astype(jnp.bfloat16)
-    back_grad = lax.all_to_all(mixed_grad, TM, split_axis=0, concat_axis=1, tiled=True)
+    back_grad = jnp.concatenate(
+        lax.all_to_all(jnp.stack(jnp.split(mixed_grad, lax.axis_size(TM), axis=0)), TM, 0, 0),
+        axis=1,
+    )
     mixed_rows = back_grad.reshape(pixels, C)
     point_part = jnp.dot(spread_low.T, mixed_rows, preferred_element_type=jnp.float32)
     spread_grad = jnp.dot(mixed_rows, point_weight.T, preferred_element_type=jnp.float32).astype(

time: 169 us -> 169 us (level)
  no operation moved by 1% of the time
where the time goes in v1:
time: 169 us; the launch traced here: 168 us
  blocking collectives  50.1 us (30%)
  starting transfers between devices  43.8 us (26%)
  local copies, waits for them, and re-layouts  32.7 us (19%)
  waiting for transfers between devices  25.4 us (15%)
  other arithmetic  8.99 us (5%)
  matrix products  5.94 us (4%)
    all_to_all x2, blocking collectives, copies(): return lax.all_to_all(wide, axis, split_axis=0, concat_axis=0, tiled=True)  21.7 us
    all_to_all x2, blocking collectives, scatter_sum(): got = lax.all_to_all(low, axis, split_axis=0, concat_axis=0, tiled=True)  20.4 us
    ppermute x2, starting transfers between devices, padded_2(): lax.ppermute(head, axis, [((i + 1) % count, i) for i in range(count)])  17 us
    all_to_all x1, starting transfers between devices, on_device(): lax.all_to_all(jnp.stack(jnp.split(mixed_grad, lax.axis_size(TM), axis=0)...  10.3 us
    all_to_all x1, waiting for transfers between devices, on_device(): lax.all_to_all(jnp.stack(jnp.split(mixed_grad, lax.axis_size(TM), axis=0)...  9.85 us
    ppermute x2, waiting for transfers between devices, padded_2(): lax.ppermute(tail, axis, [(i, (i + 1) % count) for i in range(count)])  8.5 us
    all_gather x1, blocking collectives, sum_over_devices(): rows = lax.all_gather(rows, 'core', axis=0, tiled=True)  7.96 us
    another operation x9, local copies, waits for them, and re-layouts, on_device(): taps_part = jnp.stack(taps_rows, axis=0)  7.14 us
  transfers between devices with their start and end apart: 8, of which 6 were waited for; matrix products, arithmetic and copies ran while one was open for 12% of the time, Pallas kernels for 0%

profile of v1, /device:TPU:1, one launch (start us, length us, event | category | flops | bytes accessed | tf_op | source)
XLA Modules:
  0.0 167.9 jit_solution(15891443527590837143)
XLA Ops:
  0.6 0.8 slice_bitcast_fusion.13
  1.4 1.0 convert_element_type.105
  2.8 0.8 pad_maximum_fusion.2
  3.5 10.3 %all-to-all-start = ((bf16[4,1,160,256]{3,2,1,0:T(8,128)(2,1)}), bf16[4,1,160,256]{3,2,1,0:T(8,128)(2,1)S(1)}, u32[]{:S(2)}, u32[]{:S(2)}) async-start(bf16[4,1,160,256]{3,2,1,0:T(8,128)(2,1)} %pad_maximum_fusion.2), calls=%async_computation | async-start | bytes 655360 | tf_op jit(solution)/shard_map/all_to_all | solution.py:104
  13.9 9.8 %all-to-all-done = bf16[4,1,160,256]{3,2,1,0:T(8,128)(2,1)S(1)} async-done(((bf16[4,1,160,256]{3,2,1,0:T(8,128)(2,1)}), bf16[4,1,160,256]{3,2,1,0:T(8,128)(2,1)S(1)}, u32[]{:S(2)}, u32[]{:S(2)}) %all-to-all-start) | async-done | bytes 327712 | tf_op jit(solution)/shard_map/all_to_all | solution.py:104
  24.4 0.6 fusion.12
  25.0 0.9 copy-done.2
  25.9 0.6 gather_fusion.1
  26.6 11.4 %collective-permute-start.1 = (bf16[20,1,256]{2,0,1:T(8,128)(2,1)S(1)}, bf16[20,1,256]{2,0,1:T(8,128)(2,1)S(1)}, u32[]{:S(2)}, u32[]{:S(2)}) collective-permute-start(bf16[20,1,256]{2,0,1:T(8,128)(2,1)S(1)} %fusion.49), channel_id=1, source_target_pairs={{1,0},{2,1},{3,2},{4,3},{5,4},{6,5},{7,6},{8,7},{9,8},{10,9},{11,1... | collective-permute-start | bytes 30728 | tf_op jit(solution)/shard_map/ppermute | solution.py:26
  38.0 0.6 gather_fusion
  38.6 1.9 %collective-permute-start = (bf16[20,1,256]{2,0,1:T(8,128)(2,1)S(1)}, bf16[20,1,256]{2,0,1:T(8,128)(2,1)S(1)}, u32[]{:S(2)}, u32[]{:S(2)}) collective-permute-start(bf16[20,1,256]{2,0,1:T(8,128)(2,1)S(1)} %fusion.48), channel_id=1, source_target_pairs={{0,1},{1,2},{2,3},{3,4},{4,5},{5,6},{6,7},{7,8},{8,9},{9,10},{10,1... | collective-permute-start | bytes 30728 | tf_op jit(solution)/shard_map/ppermute | solution.py:24
  40.6 1.0 copy.116
  41.6 2.5 %reshape.140 = bf16[640,1024]{1,0:T(8,128)(2,1)S(1)} reshape(bf16[1,2560,256]{2,1,0:T(8,128)(2,1)} %param.16) | data formatting | bytes 2621440 | tf_op jit(solution)/shard_map/reshape | solution.py:70
  44.1 1.2 slice.277
  45.4 3.7 %collective-permute-done = bf16[20,1,256]{2,0,1:T(8,128)(2,1)S(1)} collective-permute-done((bf16[20,1,256]{2,0,1:T(8,128)(2,1)S(1)}, bf16[20,1,256]{2,0,1:T(8,128)(2,1)S(1)}, u32[]{:S(2)}, u32[]{:S(2)}) %collective-permute-start) | collective-permute-done | bytes 10272 | tf_op jit(solution)/shard_map/ppermute | solution.py:24
  49.1 0.7 fusion.47
  50.1 0.8 fusion.38
  50.9 5.7 %collective-permute-start.3 = (bf16[1,20,1,256]{3,1,2,0:T(8,128)(2,1)S(1)}, bf16[1,20,1,256]{3,1,2,0:T(8,128)(2,1)S(1)}, u32[]{:S(2)}, u32[]{:S(2)}) collective-permute-start(bf16[1,20,1,256]{3,1,2,0:T(8,128)(2,1)S(1)} %copy.134), channel_id=1, source_target_pairs={{1,0},{2,1},{3,2},{4,3},{5,4},{6,5},{7,6},{8,7},{9,8},{10,9},{11,1... | collective-permute-start | bytes 30728 | tf_op jit(solution)/shard_map/ppermute | solution.py:26
  56.6 1.9 %collective-permute-start.2 = (bf16[1,20,1,256]{3,1,2,0:T(8,128)(2,1)S(1)}, bf16[1,20,1,256]{3,1,2,0:T(8,128)(2,1)S(1)}, u32[]{:S(2)}, u32[]{:S(2)}) collective-permute-start(bf16[1,20,1,256]{3,1,2,0:T(8,128)(2,1)S(1)} %copy.133), channel_id=1, source_target_pairs={{0,1},{1,2},{2,3},{3,4},{4,5},{5,6},{6,7},{7,8},{8,9},{9,10},{10,1... | collective-permute-start | bytes 30728 | tf_op jit(solution)/shard_map/ppermute | solution.py:24
  58.5 1.6 convolution_bitcast_fusion
  60.1 0.8 copy.129
  60.9 0.8 copy.124
  61.7 0.6 gather_fusion.3
  62.3 4.8 %collective-permute-done.2 = bf16[1,20,1,256]{3,1,2,0:T(8,128)(2,1)S(1)} collective-permute-done((bf16[1,20,1,256]{3,1,2,0:T(8,128)(2,1)S(1)}, bf16[1,20,1,256]{3,1,2,0:T(8,128)(2,1)S(1)}, u32[]{:S(2)}, u32[]{:S(2)}) %collective-permute-start.2) | collective-permute-done | bytes 10272 | tf_op jit(solution)/shard_map/ppermute | solution.py:24
  67.1 0.6 gather_fusion.2
  68.0 0.8 fusion.29
  69.0 0.5 copy.136
  69.5 0.5 broadcast.133
  70.0 3.4 %reduce.8 = bf16[640,256]{1,0:T(8,128)(2,1)} reduce(bf16[640,1,256]{2,1,0:T(2,128)(2,1)S(1)} %bitcast.117, bf16[]{:T(256)} %broadcast.133), dimensions={1}, to_apply=%bitcast.106.reduce_sub_computation | reduce | bytes 655362
  73.5 1.8 %reshape.196 = bf16[4,2,20480]{2,1,0:T(2,128)(2,1)} reshape(bf16[640,256]{1,0:T(8,128)(2,1)} %reduce.8) | data formatting | bytes 655360
  75.2 6.4 %all-to-all-start.1 = ((bf16[4,2,20480]{2,1,0:T(2,128)(2,1)}), bf16[4,2,20480]{2,1,0:T(2,128)(2,1)S(1)}, u32[]{:S(2)}, u32[]{:S(2)}) async-start(bf16[4,2,20480]{2,1,0:T(2,128)(2,1)} %reshape.196), calls=%async_computation.1 | async-start | bytes 655360 | tf_op jit(solution)/shard_map/all_to_all | solution.py:94
  81.6 0.7 fusion.37
  82.3 0.8 copy.127
  83.1 0.8 copy.128
  83.9 0.8 copy.126
  84.7 0.8 copy.122
  85.5 0.8 copy.121
  86.3 0.8 copy.120
  87.1 0.8 copy.123
  87.9 0.8 copy.125
  88.7 1.0 fusion.53
  89.7 1.7 %all-to-all-done.1 = bf16[4,2,20480]{2,1,0:T(2,128)(2,1)S(1)} async-done(((bf16[4,2,20480]{2,1,0:T(2,128)(2,1)}), bf16[4,2,20480]{2,1,0:T(2,128)(2,1)S(1)}, u32[]{:S(2)}, u32[]{:S(2)}) %all-to-all-start.1) | async-done | bytes 327712 | tf_op jit(solution)/shard_map/all_to_all | solution.py:94
  91.8 1.1 copy.115
  92.8 1.6 convolution_bitcast_fusion.1
  94.6 0.8 copy.119
  95.4 0.7 broadcast_in_dim.49
  96.1 3.0 %concatenate.24 = f32[1536,256]{0,1:T(8,128)S(1)} concatenate(f32[1024,256]{0,1:T(8,128)S(1)} %copy-done.1, f32[256,256]{0,1:T(8,128)S(1)} %copy-done.6, f32[16,256]{0,1:T(8,128)} %copy.119, f32[1,256]{0,1:T(8,128)} %copy.120, f32[1,256]{0,1:T(8,128)} %copy.121, f32[1,256]{0,1:T(8,128)} %copy.122, f32[1,256]{0,1:T(8,128)} %copy.123, f32[1,256]{0,1:T(8,128)} %copy.124, ...), dimensions={0} | concatenate | bytes 3145728 | tf_op jit(solution)/shard_map/concatenate | solution.py:147
  99.2 2.8 %collective-permute-start.4 = (bf16[768,256]{0,1:T(8,128)(2,1)S(1)}, bf16[768,256]{0,1:T(8,128)(2,1)S(1)}, u32[]{:S(2)}, u32[]{:S(2)}) collective-permute-start(bf16[768,256]{0,1:T(8,128)(2,1)S(1)} %dynamic-slice_convert_fusion), channel_id=1, source_target_pairs={{0,128},{128,0},{1,129},{129,1},{2,130},{130,2},{3,131},{131,3},{4... | collective-permute-start | bytes 1179656 | tf_op jit(solution)/shard_map/ppermute | solution.py:51
  102.0 1.3 collective-permute-done.4
  103.6 10.2 %all_to_all.42 = bf16[4,192,256]{2,1,0:T(8,128)(2,1)S(1)} all-to-all(bf16[4,192,256]{2,1,0:T(8,128)(2,1)S(1)} %bitcast.119), channel_id=1, replica_groups=mesh['yh'=2,'core'=2,'x'=4,'z'=8,'yl'=4] {'x'}, dimensions={0} | all-to-all | bytes 786432 | tf_op jit(solution)/shard_map/all_to_all | solution.py:36
  113.9 10.2 %all_to_all.43 = bf16[8,24,256]{2,1,0:T(8,128)(2,1)S(1)} all-to-all(bf16[8,24,256]{2,1,0:T(8,128)(2,1)S(1)} %bitcast.124), channel_id=1, replica_groups=mesh['yh'=2,'core'=2,'x'=4,'z'=8,'yl'=4] {'z'}, dimensions={0} | all-to-all | bytes 196608 | tf_op jit(solution)/shard_map/all_to_all | solution.py:36
  124.1 11.8 %all_to_all.44 = bf16[8,24,256]{2,1,0:T(8,128)(2,1)S(1)} all-to-all(bf16[8,24,256]{2,1,0:T(8,128)(2,1)S(1)} %broadcast_in_dim.50), channel_id=1, replica_groups=mesh['yh'=2,'core'=2,'x'=4,'z'=8,'yl'=4] {'yh','yl'}, dimensions={0} | all-to-all | bytes 196608 | tf_op jit(solution)/shard_map/all_to_all | solution.py:43
  135.9 10.0 %all_to_all.45 = bf16[8,24,256]{2,1,0:T(8,128)(2,1)S(1)} all-to-all(bf16[8,24,256]{2,1,0:T(8,128)(2,1)S(1)} %broadcast_in_dim.51), channel_id=1, replica_groups=mesh['yh'=2,'core'=2,'x'=4,'z'=8,'yl'=4] {'z'}, dimensions={0} | all-to-all | bytes 196608 | tf_op jit(solution)/shard_map/all_to_all | solution.py:43
  145.9 0.8 broadcast_in_dim.53
  146.6 3.5 %all-to-all-start.6 = ((bf16[4,192,256]{2,1,0:T(8,128)(2,1)}), bf16[4,192,256]{2,1,0:T(8,128)(2,1)S(1)}, u32[]{:S(2)}, u32[]{:S(2)}) async-start(bf16[4,192,256]{2,1,0:T(8,128)(2,1)} %broadcast_in_dim.53), calls=%async_computation.6 | async-start | bytes 786432 | tf_op jit(solution)/shard_map/all_to_all | solution.py:43
  150.1 0.5 convolution_convert_fusion
  150.7 1.6 reshape.141
  152.3 4.0 %all-to-all-done.6 = bf16[4,192,256]{2,1,0:T(8,128)(2,1)S(1)} async-done(((bf16[4,192,256]{2,1,0:T(8,128)(2,1)}), bf16[4,192,256]{2,1,0:T(8,128)(2,1)S(1)}, u32[]{:S(2)}, u32[]{:S(2)}) %all-to-all-start.6) | async-done | bytes 393248 | tf_op jit(solution)/shard_map/all_to_all | solution.py:43
  156.3 8.0 %all_gather.3 = bf16[1536,256]{1,0:T(8,128)(2,1)S(1)} all-gather(bf16[768,256]{1,0:T(8,128)(2,1)S(1)} %bitcast.120), channel_id=1, replica_groups=mesh['yh'=2,'core'=2,'x'=4,'z'=8,'yl'=4] {'core'}, dimensions={0}, use_global_device_ids=true | all-gather | bytes 1179648 | tf_op jit(solution)/shard_map/all_gather | solution.py:59
  164.4 0.6 slice.291
  165.0 0.6 slice.292
  165.6 0.7 slice.293
  166.3 1.0 slice.290
  167.3 0.6 reshape.150
  (61 shorter events, 3.2 us)
Async XLA Ops:
  0.6 49.4 %copy-start = (bf16[1024,256]{1,0:T(8,128)(2,1)S(1)}, bf16[1024,256]{1,0:T(8,128)(2,1)}, u32[]{:S(2)}) copy-start(bf16[1024,256]{1,0:T(8,128)(2,1)} %param.17) | copy-start | bytes 1572868
  2.5 11.3 %copy-start.10 = (s32[1,2,20]{2,1,0:T(2,128)S(1)}, s32[1,2,20]{2,1,0:T(2,128)}, u32[]{:S(2)}) copy-start(s32[1,2,20]{2,1,0:T(2,128)} %param.22) | copy-start | bytes 484
  2.5 11.3 %copy-start.9 = (f32[9,256]{1,0:T(8,128)S(1)}, f32[9,256]{1,0:T(8,128)}, u32[]{:S(2)}) copy-start(f32[9,256]{1,0:T(8,128)} %param.19) | copy-start | bytes 27652
  2.5 21.2 %copy-start.7 = (bf16[256,256]{1,0:T(8,128)(2,1)S(1)}, bf16[256,256]{1,0:T(8,128)(2,1)}, u32[]{:S(2)}) copy-start(bf16[256,256]{1,0:T(8,128)(2,1)} %param.20) | copy-start | bytes 393220
  3.5 20.2 %all-to-all-start = ((bf16[4,1,160,256]{3,2,1,0:T(8,128)(2,1)}), bf16[4,1,160,256]{3,2,1,0:T(8,128)(2,1)S(1)}, u32[]{:S(2)}, u32[]{:S(2)}) async-start(bf16[4,1,160,256]{3,2,1,0:T(8,128)(2,1)} %pad_maximum_fusion.2), calls=%async_computation | async-start | bytes 655360 | tf_op jit(solution)/shard_map/all_to_all | solution.py:104
  24.4 16.1 %copy-start.3 = (bf16[4,160,256]{2,1,0:T(8,128)(2,1)S(1)}, bf16[4,160,256]{2,1,0:T(8,128)(2,1)}, u32[]{:S(2)}) copy-start(bf16[4,160,256]{2,1,0:T(8,128)(2,1)} %param.23) | copy-start | bytes 983044
  25.0 0.9 copy-start.2
  26.6 18.8 %collective-permute-start.1 = (bf16[20,1,256]{2,0,1:T(8,128)(2,1)S(1)}, bf16[20,1,256]{2,0,1:T(8,128)(2,1)S(1)}, u32[]{:S(2)}, u32[]{:S(2)}) collective-permute-start(bf16[20,1,256]{2,0,1:T(8,128)(2,1)S(1)} %fusion.49), channel_id=1, source_target_pairs={{1,0},{2,1},{3,2},{4,3},{5,4},{6,5},{7,6},{8,7},{9,8},{10,9},{11,1... | collective-permute-start | bytes 30728 | tf_op jit(solution)/shard_map/ppermute | solution.py:26
  38.6 10.4 %collective-permute-start = (bf16[20,1,256]{2,0,1:T(8,128)(2,1)S(1)}, bf16[20,1,256]{2,0,1:T(8,128)(2,1)S(1)}, u32[]{:S(2)}, u32[]{:S(2)}) collective-permute-start(bf16[20,1,256]{2,0,1:T(8,128)(2,1)S(1)} %fusion.48), channel_id=1, source_target_pairs={{0,1},{1,2},{2,3},{3,4},{4,5},{5,6},{6,7},{7,8},{8,9},{9,10},{10,1... | collective-permute-start | bytes 30728 | tf_op jit(solution)/shard_map/ppermute | solution.py:24
  44.1 5.9 %copy-start.11 = (f32[256]{0:T(256)S(1)}, f32[256]{0:T(256)}, u32[]{:S(2)}) copy-start(f32[256]{0:T(256)} %param.18) | copy-start | bytes 3076
  50.8 9.3 %copy-start.4 = (bf16[640,256]{1,0:T(8,128)(2,1)}, bf16[640,256]{1,0:T(8,128)(2,1)S(1)}, u32[]{:S(2)}) copy-start(bf16[640,256]{1,0:T(8,128)(2,1)S(1)} %get-tuple-element.53) | copy-start | bytes 983044
  50.9 10.8 %collective-permute-start.3 = (bf16[1,20,1,256]{3,1,2,0:T(8,128)(2,1)S(1)}, bf16[1,20,1,256]{3,1,2,0:T(8,128)(2,1)S(1)}, u32[]{:S(2)}, u32[]{:S(2)}) collective-permute-start(bf16[1,20,1,256]{3,1,2,0:T(8,128)(2,1)S(1)} %copy.134), channel_id=1, source_target_pairs={{1,0},{2,1},{3,2},{4,3},{5,4},{6,5},{7,6},{8,7},{9,8},{10,9},{11,1... | collective-permute-start | bytes 30728 | tf_op jit(solution)/shard_map/ppermute | solution.py:26
  56.6 10.5 %collective-permute-start.2 = (bf16[1,20,1,256]{3,1,2,0:T(8,128)(2,1)S(1)}, bf16[1,20,1,256]{3,1,2,0:T(8,128)(2,1)S(1)}, u32[]{:S(2)}, u32[]{:S(2)}) collective-permute-start(bf16[1,20,1,256]{3,1,2,0:T(8,128)(2,1)S(1)} %copy.133), channel_id=1, source_target_pairs={{0,1},{1,2},{2,3},{3,4},{4,5},{5,6},{6,7},{7,8},{8,9},{9,10},{10,1... | collective-permute-start | bytes 30728 | tf_op jit(solution)/shard_map/ppermute | solution.py:24
  75.2 16.2 %all-to-all-start.1 = ((bf16[4,2,20480]{2,1,0:T(2,128)(2,1)}), bf16[4,2,20480]{2,1,0:T(2,128)(2,1)S(1)}, u32[]{:S(2)}, u32[]{:S(2)}) async-start(bf16[4,2,20480]{2,1,0:T(2,128)(2,1)} %reshape.196), calls=%async_computation.1 | async-start | bytes 655360 | tf_op jit(solution)/shard_map/all_to_all | solution.py:94
  89.7 3.1 %copy-start.8 = (bf16[4,160,256]{1,0,2:T(4,128)(2,1)S(1)}, bf16[4,160,256]{1,0,2:T(4,128)(2,1)}, u32[]{:S(2)}) copy-start(bf16[4,160,256]{1,0,2:T(4,128)(2,1)} %copy.116) | copy-start | bytes 983044
  92.8 3.3 %copy-start.1 = (f32[1024,256]{0,1:T(8,128)S(1)}, f32[1024,256]{0,1:T(8,128)}, u32[]{:S(2)}) copy-start(f32[1024,256]{0,1:T(8,128)} %convolution_bitcast_fusion) | copy-start | bytes 3145732
  92.8 3.3 %copy-start.6 = (f32[256,256]{0,1:T(8,128)S(1)}, f32[256,256]{0,1:T(8,128)}, u32[]{:S(2)}) copy-start(f32[256,256]{0,1:T(8,128)} %fusion.53) | copy-start | bytes 786436
  99.2 4.1 %collective-permute-start.4 = (bf16[768,256]{0,1:T(8,128)(2,1)S(1)}, bf16[768,256]{0,1:T(8,128)(2,1)S(1)}, u32[]{:S(2)}, u32[]{:S(2)}) collective-permute-start(bf16[768,256]{0,1:T(8,128)(2,1)S(1)} %dynamic-slice_convert_fusion), channel_id=1, source_target_pairs={{0,128},{128,0},{1,129},{129,1},{2,130},{130,2},{3,131},{131,3},{4... | collective-permute-start | bytes 1179656 | tf_op jit(solution)/shard_map/ppermute | solution.py:51
  113.8 36.3 %copy-start.5 = (bf16[640,256]{1,0:T(8,128)(2,1)S(1)}, bf16[640,256]{1,0:T(8,128)(2,1)}, u32[]{:S(2)}) copy-start(bf16[640,256]{1,0:T(8,128)(2,1)} %copy-done.4) | copy-start | bytes 983044
  146.6 9.7 %all-to-all-start.6 = ((bf16[4,192,256]{2,1,0:T(8,128)(2,1)}), bf16[4,192,256]{2,1,0:T(8,128)(2,1)S(1)}, u32[]{:S(2)}, u32[]{:S(2)}) async-start(bf16[4,192,256]{2,1,0:T(8,128)(2,1)} %broadcast_in_dim.53), calls=%async_computation.6 | async-start | bytes 786432 | tf_op jit(solution)/shard_map/all_to_all | solution.py:43
